TPU v7x, 512 devices: a whole 4x8x8 slice. The times are simulated.
512 devices in a mesh: col: 16 (over z, x_lo), row: 32 (over y, x_hi, core).
Axes of the slice: x: 4 (x_hi: 2, x_lo: 2; x = x_hi * 2 + x_lo), y: 8, z: 8, core: 2. Of those that a mesh axis runs over, the one named last changes fastest.
Arguments:
- inputs: bfloat16 [1024, 8192], P('row', 'col'), may hold values from -6 to 6
- grad_out: bfloat16 [1024, 8192], P('row', 'col'), may hold values from -6 to 6
- gate_pre: bfloat16 [1024, 16384], P('col', 'row'), may hold values from -8 to 8
- up_pre: bfloat16 [1024, 16384], P('col', 'row'), may hold values from -6 to 6
- gate_weight: bfloat16 [8192, 16384], P('col', 'row'), may hold values from -0.0625 to 0.0625
- up_weight: bfloat16 [8192, 16384], P('col', 'row'), may hold values from -0.0625 to 0.0625
- down_weight: bfloat16 [16384, 8192], P('row', 'col'), may hold values from -0.046875 to 0.046875
Outputs:
- input_grad: bfloat16 [1024, 8192], P('row', 'col')
- gate_grad: bfloat16 [8192, 16384], P('col', 'row')
- up_grad: bfloat16 [8192, 16384], P('col', 'row')
- down_grad: bfloat16 [16384, 8192], P('row', 'col')
All inputs are finite; a program needn't handle non-finite values.
Results may differ from a plain program's by a relative error of at most 0.0049.
Values may be sent and summed in bfloat16 or wider, within the bound.
A program may use at most 64 MiB of HBM per device.

v0:
```python
import math

import jax
import jax.numpy as jnp
from jax import lax
from jax.sharding import PartitionSpec as P


def swiglu_back(hidden_grad, gate_pre, up_pre):
    gate_val = gate_pre.astype(jnp.float32)
    up_val = up_pre.astype(jnp.float32)
    sigmoid_val = jax.nn.sigmoid(gate_val)
    silu_val = gate_val * sigmoid_val
    hidden = (silu_val * up_val).astype(jnp.bfloat16)
    up_term = (hidden_grad * silu_val).astype(jnp.bfloat16)
    gate_term = (
        hidden_grad * up_val * sigmoid_val * (1.0 + gate_val * (1.0 - sigmoid_val))
    ).astype(jnp.bfloat16)
    return (hidden, gate_term, up_term)


def per_device(inputs, grad_out, gate_pre, up_pre, gate_weight, up_weight, down_weight):
    total_tokens = grad_out.shape[0] * lax.axis_size("row")
    grad_scale = 1.0 / math.sqrt(total_tokens)
    grad_all, input_all = (
        lax.all_gather(grad_out, "row", axis=0, tiled=True),
        lax.all_gather(inputs, "row", axis=0, tiled=True),
    )
    partial_hidden = jnp.einsum(
        "td,fd->tf", grad_all, down_weight, preferred_element_type=jnp.float32
    )
    hidden_grad = lax.psum_scatter(partial_hidden, "col", scatter_dimension=0, tiled=True)
    hidden, gate_term, up_term = swiglu_back(hidden_grad, gate_pre, up_pre)
    hidden_all, gate_all, up_all = (
        lax.all_gather(hidden, "col", axis=0, tiled=True),
        lax.all_gather(gate_term, "col", axis=0, tiled=True),
        lax.all_gather(up_term, "col", axis=0, tiled=True),
    )
    down_grad = (
        jnp.einsum("tf,td->fd", hidden_all, grad_all, preferred_element_type=jnp.float32)
        * grad_scale
    ).astype(jnp.bfloat16)
    gate_sum = jnp.einsum("td,tf->df", input_all, gate_all, preferred_element_type=jnp.float32)
    up_sum = jnp.einsum("td,tf->df", input_all, up_all, preferred_element_type=jnp.float32)
    gate_grad = (gate_sum * grad_scale).astype(jnp.bfloat16)
    up_grad = (up_sum * grad_scale).astype(jnp.bfloat16)
    input_grad = lax.psum_scatter(
        jnp.einsum("tf,df->td", gate_all, gate_weight, preferred_element_type=jnp.float32)
        + jnp.einsum("tf,df->td", up_all, up_weight, preferred_element_type=jnp.float32),
        "row",
        scatter_dimension=0,
        tiled=True,
    ).astype(jnp.bfloat16)
    return (input_grad, gate_grad, up_grad, down_grad)


def solution(mesh):
    return jax.shard_map(
        per_device,
        mesh=mesh,
        in_specs=(
            P("row", "col"),
            P("row", "col"),
            P("col", "row"),
            P("col", "row"),
            P("col", "row"),
            P("col", "row"),
            P("row", "col"),
        ),
        out_specs=(P("row", "col"), P("col", "row"), P("col", "row"), P("row", "col")),
        check_vma=False,
    )
```

profile of v0, /device:TPU:24, one launch (start us, length us, event | category | flops | bytes accessed | tf_op | source)
XLA Modules:
  0.0 621.9 jit_solution(12379006136893260064)
XLA Ops:
  7.2 0.0 copy-start
  7.2 0.0 all-gather.6.cloned.1.call-start
  7.2 0.7 all-gather.6.cloned.1.call-update
  7.9 0.0 reduce-scatter.3.cloned.1.call-start
  8.0 89.3 %all-gather.6.cloned.1.call-done = bf16[1024,512]{1,0:T(8,128)(2,1)} async-done(((bf16[32,512]{1,0:T(8,128)(2,1)}), bf16[1024,512]{1,0:T(8,128)(2,1)}) %all-gather.6.cloned.1.call-update) | async-done | bytes 1048592 | tf_op jit(solution)/shard_map/all_gather | solution.py:26
  97.3 3.3 fusion.13
  100.6 0.0 reduce-scatter.3.cloned.1.call-update
  100.6 0.0 all-gather.8.cloned.1.call-start
  100.7 77.0 %reduce-scatter.3.cloned.1.call-done = f32[64,512]{1,0:T(8,128)} async-done(((f32[1024,512]{1,0:T(8,128)}), f32[64,512]{1,0:T(8,128)}) %reduce-scatter.3.cloned.1.call-update) | async-done | bytes 131088 | tf_op jit(solution)/shard_map/reduce_scatter | solution.py:32
  177.7 1.7 multiply_convert_fusion
  179.4 0.0 all-gather.8.cloned.1.call-update
  179.4 0.0 all-gather.10.cloned.1.call-start
  179.5 0.5 all-gather.10.cloned.1.call-update
  180.0 0.0 all-gather.12.cloned.1.call-start
  180.0 0.5 all-gather.12.cloned.1.call-update
  180.6 0.0 all-gather.14.cloned.1.call-start
  180.6 0.5 all-gather.14.cloned.1.call-update
  181.2 0.0 reduce-scatter.5.cloned.1.call-start
  181.2 69.3 %all-gather.8.cloned.1.call-done = bf16[1024,512]{1,0:T(8,128)(2,1)} async-done(((bf16[64,512]{1,0:T(8,128)(2,1)}), bf16[1024,512]{1,0:T(8,128)(2,1)}) %all-gather.8.cloned.1.call-update) | async-done | bytes 1048592 | tf_op jit(solution)/shard_map/all_gather | solution.py:36
  250.5 2.0 fusion.14
  252.5 72.7 %all-gather.10.cloned.1.call-done = bf16[1024,512]{1,0:T(8,128)(2,1)} async-done(((bf16[64,512]{1,0:T(8,128)(2,1)}), bf16[1024,512]{1,0:T(8,128)(2,1)}) %all-gather.10.cloned.1.call-update) | async-done | bytes 1048592 | tf_op jit(solution)/shard_map/all_gather | solution.py:37
  325.1 3.4 convolution_add_fusion
  328.5 0.0 reduce-scatter.5.cloned.1.call-update
  328.6 81.5 %all-gather.12.cloned.1.call-done = bf16[1024,512]{1,0:T(8,128)(2,1)} async-done(((bf16[32,512]{1,0:T(8,128)(2,1)}), bf16[1024,512]{1,0:T(8,128)(2,1)}) %all-gather.12.cloned.1.call-update) | async-done | bytes 1048592 | tf_op jit(solution)/shard_map/all_gather | solution.py:27
  410.1 2.0 fusion.4
  412.0 1.0 copy.11
  413.0 2.0 fusion.3
  415.1 1.0 copy.12
  416.1 66.3 %all-gather.14.cloned.1.call-done = bf16[1024,512]{1,0:T(8,128)(2,1)} async-done(((bf16[64,512]{1,0:T(8,128)(2,1)}), bf16[1024,512]{1,0:T(8,128)(2,1)}) %all-gather.14.cloned.1.call-update) | async-done | bytes 1048592 | tf_op jit(solution)/shard_map/all_gather | solution.py:35
  482.3 2.8 fusion.2
  485.1 128.5 %reduce-scatter.5.cloned.1.call-done = f32[32,512]{1,0:T(8,128)} async-done(((f32[1024,512]{1,0:T(8,128)}), f32[32,512]{1,0:T(8,128)}) %reduce-scatter.5.cloned.1.call-update) | async-done | bytes 65552 | tf_op jit(solution)/shard_map/reduce_scatter | solution.py:47
  613.5 1.5 convert_element_type.37
  (13 shorter events, 0.0 us)
Async XLA Ops:
  7.2 90.2 %copy-start = (bf16[512,512]{1,0:T(8,128)(2,1)S(1)}, bf16[512,512]{1,0:T(8,128)(2,1)}, u32[]{:S(2)}) copy-start(bf16[512,512]{1,0:T(8,128)(2,1)} %param.13) | copy-start | bytes 1572868
  7.2 90.1 %all-gather.6.cloned.1.call-start = ((), (), s32[]{:S(2)}) async-start(), calls=%async_computation.2 | async-start | bytes 1081344 | tf_op jit(solution)/shard_map/all_gather | solution.py:26
  7.9 169.8 %copy-start.5 = (bf16[64,512]{1,0:T(8,128)(2,1)S(1)}, bf16[64,512]{1,0:T(8,128)(2,1)}, u32[]{:S(2)}) copy-start(bf16[64,512]{1,0:T(8,128)(2,1)} %param.9) | copy-start | bytes 196612
  7.9 169.8 %copy-start.6 = (bf16[64,512]{1,0:T(8,128)(2,1)S(1)}, bf16[64,512]{1,0:T(8,128)(2,1)}, u32[]{:S(2)}) copy-start(bf16[64,512]{1,0:T(8,128)(2,1)} %param.10) | copy-start | bytes 196612
  7.9 169.8 %reduce-scatter.3.cloned.1.call-start = ((), (), s32[]{:S(2)}) async-start(), calls=%async_computation.3 | async-start | bytes 2228224 | tf_op jit(solution)/shard_map/reduce_scatter | solution.py:32
  100.6 149.9 %copy-start.4 = (bf16[512,512]{1,0:T(8,128)(2,1)S(1)}, bf16[512,512]{1,0:T(8,128)(2,1)}, u32[]{:S(2)}) copy-start(bf16[512,512]{1,0:T(8,128)(2,1)} %param.11) | copy-start | bytes 1572868
  100.6 149.8 %all-gather.8.cloned.1.call-start = ((), (), s32[]{:S(2)}) async-start(), calls=%async_computation.4 | async-start | bytes 1114112 | tf_op jit(solution)/shard_map/all_gather | solution.py:36
  179.4 145.7 %all-gather.10.cloned.1.call-start = ((), (), s32[]{:S(2)}) async-start(), calls=%async_computation.5 | async-start | bytes 1114112 | tf_op jit(solution)/shard_map/all_gather | solution.py:37
  180.0 230.1 %all-gather.12.cloned.1.call-start = ((), (), s32[]{:S(2)}) async-start(), calls=%async_computation.7 | async-start | bytes 1081344 | tf_op jit(solution)/shard_map/all_gather | solution.py:27
  180.6 301.7 %all-gather.14.cloned.1.call-start = ((), (), s32[]{:S(2)}) async-start(), calls=%async_computation.8 | async-start | bytes 1114112 | tf_op jit(solution)/shard_map/all_gather | solution.py:35
  181.2 432.4 %reduce-scatter.5.cloned.1.call-start = ((), (), s32[]{:S(2)}) async-start(), calls=%async_computation.6 | async-start | bytes 2162688 | tf_op jit(solution)/shard_map/reduce_scatter | solution.py:47
  328.5 81.5 %copy-start.2 = (bf16[1024,512]{1,0:T(8,128)(2,1)S(1)}, bf16[1024,512]{1,0:T(8,128)(2,1)}, u32[]{:S(2)}) copy-start(bf16[1024,512]{1,0:T(8,128)(2,1)} %all-gather.8.cloned.1.call-done) | copy-start | bytes 3145732
  328.6 84.5 %copy-start.3 = (bf16[1024,512]{1,0:T(8,128)(2,1)S(1)}, bf16[1024,512]{1,0:T(8,128)(2,1)}, u32[]{:S(2)}) copy-start(bf16[1024,512]{1,0:T(8,128)(2,1)} %all-gather.10.cloned.1.call-done) | copy-start | bytes 3145732
  413.0 69.3 %copy-start.1 = (bf16[1024,512]{1,0:T(8,128)(2,1)S(1)}, bf16[1024,512]{1,0:T(8,128)(2,1)}, u32[]{:S(2)}) copy-start(bf16[1024,512]{1,0:T(8,128)(2,1)} %all-gather.6.cloned.1.call-done) | copy-start | bytes 3145732
Sparse Core Ops, SparseCore 0:
  11.4 85.8 all-gather.5
  100.8 76.9 reduce-scatter.2
  180.4 70.0 all-gather.7
  253.0 72.0 all-gather.9
  328.3 81.6 all-gather.11
  412.0 70.3 all-gather.13
  487.1 126.4 reduce-scatter.4
where the time goes:
time: 623 us; the launch traced here: 622 us
  waiting for transfers between devices  587 us (94%)
  matrix products  15.4 us (2%)
  between operations  14.2 us (2%)
    reduce_scatter x1, waiting for transfers between devices, per_device(): lax.psum_scatter(jnp.einsum('tf,df->td', gate_all, gate_weight, preferred...  128 us
    all_gather x1, waiting for transfers between devices, per_device(): lax.all_gather(grad_out, 'row', axis=0, tiled=True)  89.3 us
    all_gather x1, waiting for transfers between devices, per_device(): lax.all_gather(inputs, 'row', axis=0, tiled=True)  81.5 us
    reduce_scatter x1, waiting for transfers between devices, per_device(): lax.psum_scatter(partial_hidden, 'col', scatter_dimension=0, tiled=True)  77 us
    all_gather x1, waiting for transfers between devices, per_device(): lax.all_gather(up_term, 'col', axis=0, tiled=True)  72.7 us
    all_gather x1, waiting for transfers between devices, per_device(): lax.all_gather(gate_term, 'col', axis=0, tiled=True)  69.3 us
    all_gather x1, waiting for transfers between devices, per_device(): lax.all_gather(hidden, 'col', axis=0, tiled=True)  66.3 us
  transfers between devices with their start and end apart: 7, of which 7 were waited for; matrix products, arithmetic and copies ran while one was open for 2% of the time, Pallas kernels for 0%

commit v1 on v0

v1 whole, which is shorter than its diff:
```python
import functools
import math

import jax
import jax.numpy as jnp
from jax import lax
from jax.experimental import pallas as pl
from jax.experimental.pallas import tpu as pltpu
from jax.sharding import PartitionSpec as P

MESH = pl.DeviceIdType.MESH
F32 = jnp.float32
BF16 = jnp.bfloat16


def mod8(v):
    return lax.rem(v + 16, 8)


def kernel(
    scale, inp, gout, gpre, upre, gw, uw, dw,
    o_ig, o_gg, o_ug, o_dg,
    G, X, PRE, A, B, HID, dwt, gwt, uwt, PH, rs_s, rs_r, rl_s, rl_r, xs, xr, S,
    HG, TG, TU, IG, IGR, ES, ER, ACC, fs, fr, ss, rs,
):
    col = lax.axis_index("col")
    row = lax.axis_index("row")
    z, xl = lax.div(col, 2), lax.rem(col, 2)
    y, xh, co = lax.div(row, 4), lax.rem(lax.div(row, 2), 2), lax.rem(row, 2)

    def at_z(zz):
        return {"col": zz * 2 + xl, "row": row}

    def at_y(yy):
        return {"col": col, "row": yy * 4 + xh * 2 + co}

    zdev = {1: at_z(mod8(z + 1)), -1: at_z(mod8(z - 1))}
    xlo = {"col": z * 2 + 1 - xl, "row": row}
    xhi = {"col": col, "row": y * 4 + (1 - xh) * 2 + co}
    sib = {"col": col, "row": y * 4 + xh * 2 + 1 - co}
    ypeer = {d: at_y(mod8(y + d)) for d in range(1, 8)}

    names = {}
    sends = []

    def sem(name):
        return names.setdefault(name, len(names))

    def send(name, src, dst, dev):
        i = sem(name)
        c = pltpu.make_async_remote_copy(
            src_ref=src, dst_ref=dst, send_sem=ss.at[i], recv_sem=rs.at[i],
            device_id=dev, device_id_type=MESH,
        )
        c.start()
        sends.append(c)

    def recv(name, dst):
        i = sem(name)
        pltpu.make_async_remote_copy(
            src_ref=dst, dst_ref=dst, send_sem=ss.at[i], recv_sem=rs.at[i],
            device_id=sib, device_id_type=MESH,
        ).wait_recv()

    bar = pltpu.get_barrier_semaphore()
    partners = [zdev[1], zdev[-1], xlo, xhi, sib] + [ypeer[d] for d in range(1, 8)]
    for dev in partners:
        pl.semaphore_signal(bar, inc=1, device_id=dev, device_id_type=MESH)
    G[y, xh, co] = gout[...]
    X[y, xh, co] = inp[...]
    PRE[0, z, xl] = gpre[...]
    PRE[1, z, xl] = upre[...]
    dwt[...] = dw[...].T
    gwt[...] = gw[...].T
    uwt[...] = uw[...].T
    pl.semaphore_wait(bar, len(partners))

    yorder = [4, 3, 5, 2, 6, 1, 7]
    own = G.at[y, xh, co]
    for d in yorder:
        send(f"gy{d}", own, own, ypeer[d])
    send("gx0", own, own, xhi)

    def pre_send(s, k):
        blk = PRE.at[:, mod8(z - s * (k - 1)), xl]
        send(f"pz{s}{k}", blk, blk, zdev[s])

    def pre_x(tag, zz):
        blk = PRE.at[:, zz, xl]
        send(f"px{tag}", blk, blk, xlo)

    def pre_recv(s, k):
        recv(f"pz{s}{k}", PRE.at[:, mod8(z - s * k), xl])

    pre_send(1, 1)
    pre_send(-1, 1)
    pre_x("0", z)

    def gy_fwd(d):
        blk = G.at[mod8(y - d), xh, co]
        recv(f"gy{d}", blk)
        send(f"gx{d}", blk, blk, xhi)

    def pre_hop(k):
        for s in (1, -1):
            if s == 1 or k < 4:
                pre_recv(s, k)
                if k < (4 if s == 1 else 3):
                    pre_send(s, k + 1)
                pre_x(f"{s}{k}", mod8(z - s * k))

    gy_fwd(1)
    gy_fwd(7)
    gy_fwd(2)
    gy_fwd(6)
    pre_hop(1)
    gy_fwd(3)
    gy_fwd(5)
    gy_fwd(4)
    send("gs0", G.at[:, xh, co], G.at[:, xh, co], sib)
    pre_hop(2)
    for d in [0, 1, 7, 2, 6, 3, 5, 4]:
        recv(f"gx{d}", G.at[mod8(y - d), 1 - xh, co])
    send("gs1", G.at[:, 1 - xh, co], G.at[:, 1 - xh, co], sib)
    xown = X.at[y, xh, co]
    recv("gs0", G.at[:, xh, 1 - co])
    recv("gs1", G.at[:, 1 - xh, 1 - co])

    def partial(t):
        g = G[t].reshape(128, 512)
        PH[t] = jnp.dot(g, dwt[...], preferred_element_type=F32)

    streams = [(0, 1), (0, -1), (1, 1), (1, -1)]

    def hops(h, s):
        return 4 if (h == 0) == (s == 1) else 3

    def half(h):
        return pl.ds(h * 256, 256)

    def rs_step(h, s, k):
        n = hops(h, s)
        i = streams.index((h, s))
        t = mod8(z + s * (n - k + 1))
        val = PH[t, :, half(h)]
        if k > 1:
            recv(f"r{i}{k - 1}", rs_r.at[i, k - 1])
            val = val + rs_r[i, k - 1].astype(F32)
        if k == n:
            rl_s[i] = val
            send(f"r{i}{k}", rl_s.at[i], rl_r.at[i], zdev[s])
        else:
            rs_s[i, k] = val.astype(BF16)
            send(f"r{i}{k}", rs_s.at[i, k], rs_r.at[i, k], zdev[s])

    def terms(t):
        for h in (0, 1):
            g = PRE[0, t, :, :, half(h)].reshape(128, 256).astype(F32)
            u = PRE[1, t, :, :, half(h)].reshape(128, 256).astype(F32)
            sg = 1.0 / (1.0 + jnp.exp(-g))
            silu = g * sg
            A[t, :, half(h)] = silu
            HID[t, :, half(h)] = (silu * u).astype(BF16)
            B[t, :, half(h)] = u * sg * (1.0 + g * (1.0 - sg))

    def got_x(tag, zz):
        recv(f"px{tag}", PRE.at[:, zz, 1 - xl])

    partial(mod8(z + 4))
    rs_step(0, 1, 1)
    rs_step(1, -1, 1)
    partial(mod8(z + 3))
    partial(mod8(z - 3))
    rs_step(0, -1, 1)
    rs_step(1, 1, 1)
    for d in yorder:
        send(f"xy{d}", xown, xown, ypeer[d])
    for d in (2, -2, 1, -1, 0):
        partial(mod8(z + d))
    pre_hop(3)
    for i, (h, s) in enumerate(streams):
        if hops(h, s) == 4:
            rs_step(h, s, 2)
    for i, (h, s) in enumerate(streams):
        if hops(h, s) == 3:
            rs_step(h, s, 2)
    got_x("0", z)
    terms(z)
    got_x("11", mod8(z - 1))
    terms(mod8(z - 1))
    got_x("-11", mod8(z + 1))
    terms(mod8(z + 1))
    for want in (4, 3):
        for h, s in streams:
            if hops(h, s) == want:
                rs_step(h, s, 3)
    pre_hop(4)
    got_x("12", mod8(z - 2))
    terms(mod8(z - 2))
    got_x("-12", mod8(z + 2))
    terms(mod8(z + 2))
    for h, s in streams:
        if hops(h, s) == 4:
            rs_step(h, s, 4)
    S[...] = PH[z]
    for want in (3, 4):
        for i, (h, s) in enumerate(streams):
            n = hops(h, s)
            if n == want:
                recv(f"r{i}{n}", rl_r.at[i])
                S[:, half(h)] = S[:, half(h)] + rl_r[i]

    xs[...] = S[...].astype(BF16)
    send("xs", xs, xr, xlo)
    for tag, d in (("13", -3), ("-13", 3), ("14", 4)):
        got_x(tag, mod8(z + d))
        terms(mod8(z + d))
    recv("xs", xr)
    own_hg = (S[...] + xr[...].astype(F32)).astype(BF16)
    HG[z, 0] = own_hg[:, :256]
    HG[z, 1] = own_hg[:, 256:]

    def hg_send(h, s, k):
        blk = HG.at[mod8(z - s * (k - 1)), h]
        send(f"h{streams.index((h, s))}{k}", blk, blk, zdev[s])

    def hg_recv(h, s, k):
        recv(f"h{streams.index((h, s))}{k}", HG.at[mod8(z - s * k), h])

    for h, s in streams:
        hg_send(h, s, 1)

    def block(slot, t):
        for h in (0, 1):
            hg = HG[t, h].astype(F32)
            TG[t, :, half(h)] = (hg * B[t, :, half(h)]).astype(BF16)
            TU[t, :, half(h)] = (hg * A[t, :, half(h)]).astype(BF16)
        val = jnp.dot(TG[t], gwt[...], preferred_element_type=F32) + jnp.dot(
            TU[t], uwt[...], preferred_element_type=F32
        )
        IG[slot] = val.reshape(2, 2, 32, 512)
        send(f"c{slot}", IG.at[slot, :, 1 - co], IGR.at[slot], sib)

    def out_block(slot, t):
        recv(f"c{slot}", IGR.at[slot])
        val = IG[slot, :, co] + IGR[slot]

        @pl.when(t == y)
        def _():
            ACC[...] = val

        @pl.when(t != y)
        def _():
            ES[slot] = val.astype(BF16)
            e_copy(slot, t).start()

    def e_copy(slot, t):
        d = mod8(t - y)
        return pltpu.make_async_remote_copy(
            src_ref=ES.at[slot], dst_ref=ER.at[d], send_sem=ss.at[e0 + slot], recv_sem=rs.at[e0 + d],
            device_id=at_y(t), device_id_type=MESH,
        )

    e0 = 112
    slots = [0, -1, 1, -2, 2, -3, 3, 4]

    def grads(lhs, rhs, out):
        def body(i, carry):
            rows = pl.ds(pl.multiple_of(i * 128, 128), 128)
            a = lhs(rows)
            acc = lax.dot_general(a, rhs(), (((0,), (0,)), ((), ())), preferred_element_type=F32)
            out[rows, :] = (acc * scale).astype(BF16)
            return carry

        lax.fori_loop(0, 4, body, 0)

    block(0, z)
    for d in range(1, 8):
        recv(f"xy{d}", X.at[mod8(y - d), xh, co])
    send("xx", X.at[:, xh, co], X.at[:, xh, co], xhi)
    for k in (1, 2, 3, 4):
        for h, s in streams:
            if k <= hops(h, s):
                hg_recv(h, s, k)
                if k < hops(h, s):
                    hg_send(h, s, k + 1)
        if k < 4:
            block(2 * k - 1, mod8(z - k))
            block(2 * k, mod8(z + k))
        else:
            block(7, mod8(z + 4))
        if k == 1:
            out_block(0, z)
            grads(
                lambda rows: HID[:, :, rows].reshape(1024, 128),
                lambda: G[...].reshape(1024, 512),
                o_dg,
            )
        else:
            out_block(2 * k - 3, mod8(z - k + 1))
            out_block(2 * k - 2, mod8(z + k - 1))
        if k == 3:
            recv("xx", X.at[:, 1 - xh, co])
            send("xc", X.at[:, :, co], X.at[:, :, co], sib)
    out_block(7, mod8(z + 4))

    recv("xc", X.at[:, :, 1 - co])
    x_rows = lambda rows: X[:, :, :, :, rows].reshape(1024, 128)
    grads(x_rows, lambda: TG[...].reshape(1024, 512), o_gg)
    for d in range(1, 8):
        i = e0 + d
        pltpu.make_async_remote_copy(
            src_ref=ER.at[d], dst_ref=ER.at[d], send_sem=ss.at[i], recv_sem=rs.at[i],
            device_id=sib, device_id_type=MESH,
        ).wait_recv()
        ACC[...] = ACC[...] + ER[d].astype(F32)
    fs[...] = ACC[1 - xh]
    send("f", fs, fr, xhi)
    grads(x_rows, lambda: TU[...].reshape(1024, 512), o_ug)
    recv("f", fr)
    o_ig[...] = (ACC[xh] + fr[...]).astype(BF16)

    for c in sends:
        c.wait_send()
    for slot, d in enumerate(slots):
        t = mod8(z + d)

        @pl.when(t != y)
        def _():
            e_copy(slot, t).wait_send()

    assert len(names) <= e0


def per_device(inputs, grad_out, gate_pre, up_pre, gate_weight, up_weight, down_weight):
    scale = 1.0 / math.sqrt(grad_out.shape[0] * lax.axis_size("row"))
    vm = pltpu.VMEM
    return pl.pallas_call(
        functools.partial(kernel, scale),
        out_shape=(
            jax.ShapeDtypeStruct((32, 512), BF16),
            jax.ShapeDtypeStruct((512, 512), BF16),
            jax.ShapeDtypeStruct((512, 512), BF16),
            jax.ShapeDtypeStruct((512, 512), BF16),
        ),
        in_specs=[pl.BlockSpec(memory_space=vm)] * 7,
        out_specs=[pl.BlockSpec(memory_space=vm)] * 4,
        scratch_shapes=[
            vm((8, 2, 2, 32, 512), BF16),
            vm((8, 2, 2, 32, 512), BF16),
            vm((2, 8, 2, 64, 512), BF16),
            vm((8, 128, 512), F32),
            vm((8, 128, 512), F32),
            vm((8, 128, 512), BF16),
            vm((512, 512), BF16),
            vm((512, 512), BF16),
            vm((512, 512), BF16),
            vm((8, 128, 512), F32),
            vm((4, 4, 128, 256), BF16),
            vm((4, 4, 128, 256), BF16),
            vm((4, 128, 256), F32),
            vm((4, 128, 256), F32),
            vm((128, 512), BF16),
            vm((128, 512), BF16),
            vm((128, 512), F32),
            vm((8, 2, 128, 256), BF16),
            vm((8, 128, 512), BF16),
            vm((8, 128, 512), BF16),
            vm((8, 2, 2, 32, 512), F32),
            vm((8, 2, 32, 512), F32),
            vm((8, 2, 32, 512), BF16),
            vm((8, 2, 32, 512), BF16),
            vm((2, 32, 512), F32),
            vm((32, 512), F32),
            vm((32, 512), F32),
            pltpu.SemaphoreType.DMA((120,)),
            pltpu.SemaphoreType.DMA((120,)),
        ],
        compiler_params=pltpu.CompilerParams(
            collective_id=0, has_side_effects=True, vmem_limit_bytes=56 * 1024 * 1024
        ),
        name="swiglu_backward",
    )(inputs, grad_out, gate_pre, up_pre, gate_weight, up_weight, down_weight)


def solution(mesh):
    return jax.shard_map(
        per_device,
        mesh=mesh,
        in_specs=(
            P("row", "col"),
            P("row", "col"),
            P("col", "row"),
            P("col", "row"),
            P("col", "row"),
            P("col", "row"),
            P("row", "col"),
        ),
        out_specs=(P("row", "col"), P("col", "row"), P("col", "row"), P("row", "col")),
        check_vma=False,
    )
```

time: 623 us -> 102 us (0.16)
  waiting for transfers between devices: 587 us -> 0 us
  Pallas kernels: 0 us -> 95.5 us
  matrix products: 15.4 us -> 0 us
  between operations: 14.2 us -> 0.64 us
    all_gather x5 -> x0, waiting for transfers between devices: 379 us -> none  [the longest x1 89.3 us: per_device(): lax.all_gather(grad_out, 'row', axis=0, tiled=True)]
    reduce_scatter x2 -> x0, waiting for transfers between devices: 205 us -> none  [the longest x1 128 us: per_device(): lax.psum_scatter(jnp.einsum('tf,df->td', gate_all, gate_weight, preferred...]
    pallas_call x0 -> x1, Pallas kernels: none -> 95.5 us  [per_device(): pl.pallas_call(functools.partial(kernel, scale), out_shape=(jax.ShapeDtyp...]
    dot_general x6 -> x0, matrix products: 15.4 us -> none  [the longest x1 3.42 us: per_device(): jnp.einsum('tf,df->td', up_all, up_weight, preferred_element_type=jnp.flo...]
  transfers between devices with their start and end apart: 7 -> 0, of which waited for: 7 -> 0; matrix products, arithmetic and copies ran while one was open for 2% -> 0% of each run, Pallas kernels for 0% -> 0%
where the time goes in v1:
time: 102 us; the launch traced here: 101 us
  Pallas kernels  95.5 us (94%)
  local copies, waits for them, and re-layouts  5.33 us (5%)
    pallas_call x1, Pallas kernels, per_device(): pl.pallas_call(functools.partial(kernel, scale), out_shape=(jax.ShapeDtyp...  95.5 us
    unnamed x8, local copies, waits for them, and re-layouts  5.33 us

profile of v1, /device:TPU:24, one launch (start us, length us, event | category | flops | bytes accessed | tf_op | source)
XLA Modules:
  0.0 101.5 jit_solution(5870126898697187653)
XLA Ops:
  0.6 95.5 %swiglu_backward.1 = (bf16[32,512]{1,0:T(8,128)(2,1)}, bf16[512,512]{1,0:T(8,128)(2,1)}, bf16[512,512]{1,0:T(8,128)(2,1)}, bf16[512,512]{1,0:T(8,128)(2,1)}) custom-call(bf16[32,512]{1,0:T(8,128)(2,1)} %inp.1, bf16[32,512]{1,0:T(8,128)(2,1)} %gout.1, bf16[64,512]{1,0:T(8,128)(2,1)} %gpre.1, bf16[64,512]{1,0:T(8,128)(2,1)} %upre.1, bf16[512,512]{1,0:T(8,128)(2,1)} %gw.1, ...), custom_call_target="tpu_custom_call" | custom-call | tf_op jit(solution)/shard_map/swiglu_backward/pallas_call | solution.py:338
  96.1 1.4 %copy.15 = bf16[32,512]{1,0:T(8,128)(2,1)} copy(bf16[32,512]{1,0:T(8,128)(2,1)} %get-tuple-element.8) | data formatting | bytes 65536
  97.5 0.0 copy-start.1
  97.5 1.9 %copy.16 = bf16[512,512]{1,0:T(8,128)(2,1)} copy(bf16[512,512]{1,0:T(8,128)(2,1)} %get-tuple-element.9) | data formatting | bytes 1048576
  99.4 0.0 copy-done.1
  99.4 0.0 copy-start
  99.4 0.8 copy.17
  100.2 0.4 copy-done
  100.7 0.8 copy.18
Async XLA Ops:
  97.5 1.9 %copy-start.1 = (bf16[512,512]{1,0:T(8,128)(2,1)S(1)}, bf16[512,512]{1,0:T(8,128)(2,1)}, u32[]{:S(2)}) copy-start(bf16[512,512]{1,0:T(8,128)(2,1)} %get-tuple-element.10) | copy-start | bytes 1572868
  99.4 1.2 %copy-start = (bf16[512,512]{1,0:T(8,128)(2,1)S(1)}, bf16[512,512]{1,0:T(8,128)(2,1)}, u32[]{:S(2)}) copy-start(bf16[512,512]{1,0:T(8,128)(2,1)} %get-tuple-element.11) | copy-start | bytes 1572868

commit v2 on v0

v2 whole, which is shorter than its diff:
```python
import functools
import math

import jax
import jax.numpy as jnp
from jax import lax
from jax.experimental import pallas as pl
from jax.experimental.pallas import tpu as pltpu
from jax.sharding import PartitionSpec as P

MESH = pl.DeviceIdType.MESH
F32 = jnp.float32
BF16 = jnp.bfloat16
SEMS = 124


def mod8(v):
    return lax.rem(v + 16, 8)


def kernel(
    scale, inp, gout, gpre, upre, gw, uw, dw,
    o_ig, o_gg, o_ug, o_dg,
    G, X, PRE, A, B, HID, dwt, gwt, uwt, PH, rs_s, rs_r, rl_s, rl_r, xs, xr, S,
    HG, TG, TU, IG, IGR, ES, ER, ACC, vig, vgg, vug, vdg, vgw, vuw, vdw, ss, rs, ls,
):
    col = lax.axis_index("col")
    row = lax.axis_index("row")
    z, xl = lax.div(col, 2), lax.rem(col, 2)
    y, xh, co = lax.div(row, 4), lax.rem(lax.div(row, 2), 2), lax.rem(row, 2)

    def at_z(zz):
        return {"col": zz * 2 + xl, "row": row}

    def at_y(yy, x=None):
        return {"col": col, "row": yy * 4 + (xh if x is None else x) * 2 + co}

    zdev = {1: at_z(mod8(z + 1)), -1: at_z(mod8(z - 1))}
    xlo = {"col": z * 2 + 1 - xl, "row": row}
    xhi = at_y(y, 1 - xh)
    sib = {"col": col, "row": y * 4 + xh * 2 + 1 - co}

    names = {}

    def sem(name):
        return names.setdefault(name, len(names))

    def copy(src, dst, i, j, dev):
        return pltpu.make_async_remote_copy(
            src_ref=src, dst_ref=dst, send_sem=ss.at[i], recv_sem=rs.at[j],
            device_id=dev, device_id_type=MESH,
        )

    groups = {"g": 0, "x": 0, "p": 1, "s": 1, "v": 2, "w": 3, "e": 4, "h": 5, "r": 6, "l": 7, "c": 8}

    def send(name, src, dst, dev):
        copy(src, dst, groups[name[0]], sem(name), dev).start()

    def sent(group, ref):
        i = groups[group]
        copy(ref, ref, i, 0, sib).wait_send()

    def recv_at(i, dst):
        copy(dst, dst, i, i, sib).wait_recv()

    def recv(name, dst):
        recv_at(sem(name), dst)

    bar = pltpu.get_barrier_semaphore()
    partners = [zdev[1], zdev[-1], xlo, xhi, sib]
    partners += [at_y(mod8(y + d)) for d in range(1, 8)]
    partners += [at_y(mod8(y + d), 1 - xh) for d in range(1, 8)]
    for dev in partners:
        pl.semaphore_signal(bar, inc=1, device_id=dev, device_id_type=MESH)
    loads = [
        pltpu.make_async_copy(a, b, ls.at[4 + i])
        for i, (a, b) in enumerate(
            (
                (gout, G.at[y, xh, co]),
                (gpre, PRE.at[0, z, xl]),
                (upre, PRE.at[1, z, xl]),
                (inp, X.at[y, xh, co]),
                (dw, vdw),
                (gw, vgw),
                (uw, vuw),
            )
        )
    ]
    for c in loads:
        c.start()
    for c in loads[:4]:
        c.wait()
    pl.semaphore_wait(bar, len(partners))

    yorder = [4, 3, 5, 2, 6, 1, 7]
    need = [4, 3, -3, 2, -2, 1, -1, 0]
    own = G.at[y, xh, co]
    g0 = [sem(f"gy{d}") for d in range(8)][0]
    for d in yorder:
        send(f"gy{d}", own, own, at_y(mod8(y + d)))

    def pre_hops(a, s):
        return 4 if (a == 0) == (s == 1) else 3

    def pre_send(a, s, k):
        blk = PRE.at[a, mod8(z - s * (k - 1)), xl]
        send(f"pz{a}{s}{k}", blk, blk, zdev[s])

    def pre_x(d):
        blk = PRE.at[:, mod8(z + d), xl]
        send(f"px{d}", blk, blk, xlo)

    def pre_hop(k):
        for a in (0, 1):
            for s in (1, -1):
                n = pre_hops(a, s)
                if k <= n:
                    recv(f"pz{a}{s}{k}", PRE.at[a, mod8(z - s * k), xl])
                if k < n:
                    pre_send(a, s, k + 1)

    for a in (0, 1):
        for s in (1, -1):
            pre_send(a, s, 1)

    def g_row(j):
        t = mod8(z + j)
        d = mod8(y - t)

        @pl.when(d != 0)
        def _():
            recv_at(g0 + d, G.at[t, xh, co])

        blk = G.at[t, xh, co]
        send(f"gx{j}", blk, blk, xhi)

    def g_sib(j):
        t = mod8(z + j)
        recv(f"gx{j}", G.at[t, 1 - xh, co])
        blk = G.at[t, :, co]
        send(f"gs{j}", blk, blk, sib)

    def partial(j):
        t = mod8(z + j)
        recv(f"gs{j}", G.at[t, :, 1 - co])
        PH[t] = jnp.dot(G[t].reshape(128, 512), dwt[...], preferred_element_type=F32)

    xown = X.at[y, xh, co]
    send("xx", xown, xown, xhi)
    pre_x(0)
    for c, v, t in zip(loads[4:], (vdw, vgw, vuw), (dwt, gwt, uwt)):
        c.wait()
        t[...] = v[...].T
    g_row(4)
    pre_hop(1)
    for j in need[1:]:
        g_row(j)
    pre_x(-1)
    pre_x(1)
    for j in need[:3]:
        g_sib(j)

    slices = [0, 1, 2, 3]

    def hops(q, s):
        return 4 if (q < 2) == (s == 1) else 3

    streams = [(q, s) for n in (4, 3) for q in slices for s in (1, -1) if hops(q, s) == n]

    def cols(q):
        return pl.ds(q * 128, 128)

    def rs_step(q, s, k):
        n = hops(q, s)
        i = streams.index((q, s))
        t = mod8(z + s * (n - k + 1))
        val = PH[t, :, cols(q)]
        if k > 1:
            recv(f"r{i}{k - 1}", rs_r.at[i, k - 1])
            val = val + rs_r[i, k - 1].astype(F32)
        if k == n:
            rl_s[i] = val
            send(f"l{i}", rl_s.at[i], rl_r.at[i], zdev[s])
        else:
            rs_s[i, k] = val.astype(BF16)
            send(f"r{i}{k}", rs_s.at[i, k], rs_r.at[i, k], zdev[s])

    def rs_all(n, k):
        for q, s in streams:
            if hops(q, s) == n:
                rs_step(q, s, k)

    def terms(j):
        t = mod8(z + j)
        recv(f"px{j}", PRE.at[:, t, 1 - xl])
        for h in (0, 1):
            c = pl.ds(h * 256, 256)
            g = PRE[0, t, :, :, c].reshape(128, 256).astype(F32)
            u = PRE[1, t, :, :, c].reshape(128, 256).astype(F32)
            sg = 1.0 / (1.0 + jnp.exp(-g))
            silu = g * sg
            A[t, :, c] = silu
            HID[t, :, c] = (silu * u).astype(BF16)
            B[t, :, c] = u * sg * (1.0 + g * (1.0 - sg))

    partial(4)
    rs_all(4, 1)
    partial(3)
    partial(-3)
    rs_all(3, 1)
    pre_hop(2)
    g_sib(2)
    g_sib(-2)
    rs_all(4, 2)
    partial(2)
    partial(-2)
    rs_all(3, 2)
    for j in (1, -1, 0):
        g_sib(j)
    pre_x(-2)
    pre_x(2)
    recv("xx", X.at[y, 1 - xh, co])
    xpair = X.at[y, :, co]
    for d in yorder:
        copy(xpair, xpair, groups["v"], sem("v"), at_y(mod8(y + d))).start()
    pre_hop(3)
    rs_all(4, 3)
    partial(1)
    partial(-1)
    rs_all(3, 3)
    terms(0)
    rs_all(4, 4)
    partial(0)
    pre_hop(4)
    for q in slices:
        val = PH[z, :, cols(q)]
        for s in (1, -1):
            n = hops(q, s)
            i = streams.index((q, s))
            recv(f"l{i}", rl_r.at[i])
            val = val + rl_r[i]
        S[q] = val
        xs[q] = val.astype(BF16)
        send(f"s{q}", xs.at[q], xr.at[q], xlo)

    def hg_send(q, s, k):
        blk = HG.at[mod8(z - s * (k - 1)), q]
        send(f"h{streams.index((q, s))}{k}", blk, blk, zdev[s])

    for q in slices:
        recv(f"s{q}", xr.at[q])
        HG[z, q] = (S[q] + xr[q].astype(F32)).astype(BF16)
        hg_send(q, 1, 1)
        hg_send(q, -1, 1)
    for d in (-3, 3, 4):
        pre_x(d)

    def block(slot, j):
        t = mod8(z + j)
        for q in slices:
            hg = HG[t, q].astype(F32)
            TG[t, :, cols(q)] = (hg * B[t, :, cols(q)]).astype(BF16)
            TU[t, :, cols(q)] = (hg * A[t, :, cols(q)]).astype(BF16)
        val = jnp.dot(TG[t], gwt[...], preferred_element_type=F32) + jnp.dot(
            TU[t], uwt[...], preferred_element_type=F32
        )
        IG[slot] = val.reshape(2, 2, 32, 512)
        send(f"c{slot}", IG.at[slot, :, 1 - co], IGR.at[slot], sib)


    def e_copy(slot, j, other):
        t = mod8(z + j)
        d = mod8(t - y)
        return copy(
            ES.at[8 * other + slot], ER.at[8 * other + d], groups["e"], sem("e"),
            at_y(t, 1 - xh if other else xh),
        )

    def out_block(slot, j):
        t = mod8(z + j)
        recv(f"c{slot}", IGR.at[slot])
        ES[8 + slot] = (IG[slot, 1 - xh, co] + IGR[slot, 1 - xh]).astype(BF16)
        e_copy(slot, j, 1).start()
        val = IG[slot, xh, co] + IGR[slot, xh]

        @pl.when(t == y)
        def _():
            ACC[...] = val

        @pl.when(t != y)
        def _():
            ES[slot] = val.astype(BF16)
            e_copy(slot, j, 0).start()

    order = [0, -1, 1, -2, 2, -3, 3, 4]

    def grads(lhs, rhs, vout, out, i):
        def body(n, carry):
            rows = pl.ds(pl.multiple_of(n * 128, 128), 128)
            acc = lax.dot_general(
                lhs(rows), rhs(), (((0,), (0,)), ((), ())), preferred_element_type=F32
            )
            vout[rows, :] = (acc * scale).astype(BF16)
            return carry

        lax.fori_loop(0, 4, body, 0)
        pltpu.make_async_copy(vout, out, ls.at[i]).start()

    block(0, 0)
    for k in (1, 2, 3, 4):
        for q, s in streams:
            if k <= hops(q, s):
                recv(f"h{streams.index((q, s))}{k}", HG.at[mod8(z - s * k), q])
                if k < hops(q, s):
                    hg_send(q, s, k + 1)
        mine = (-k, k) if k < 4 else (4,)
        for j in mine:
            terms(j)
        for j in mine:
            block(order.index(j), j)
        for j in (0,) if k == 1 else (1 - k, k - 1):
            out_block(order.index(j), j)
        if k == 3:
            recv("v", X.at[pl.ds(0, 7), 0])
            send("w", X.at[:, :, co], X.at[:, :, co], sib)
    out_block(7, 4)

    x_rows = lambda rows: X[:, :, :, :, rows].reshape(1024, 128)
    h_rows = lambda rows: HID[:, :, rows].reshape(1024, 128)
    grads(h_rows, lambda: G[...].reshape(1024, 512), vdg, o_dg, 0)
    recv("w", X.at[:, :, 1 - co])
    grads(x_rows, lambda: TG[...].reshape(1024, 512), vgg, o_gg, 1)
    grads(x_rows, lambda: TU[...].reshape(1024, 512), vug, o_ug, 2)
    recv("e", ER.at[pl.ds(1, 15)])
    total = ACC[...]
    for i in range(1, 16):
        total = total + ER[i].astype(F32)
    vig[...] = total.astype(BF16)
    pltpu.make_async_copy(vig, o_ig, ls.at[3]).start()

    sent("g", G)
    sent("p", PRE)
    sent("v", X.at[pl.ds(0, 7), 0])
    sent("w", X.at[pl.ds(0, 4)])
    sent("e", ES.at[pl.ds(0, 15)])
    sent("h", HG.at[pl.ds(0, 7)])
    sent("r", rs_s.at[pl.ds(0, 5)])
    sent("l", rl_s)
    sent("c", IGR)
    for i, (v, o) in enumerate(((vdg, o_dg), (vgg, o_gg), (vug, o_ug), (vig, o_ig))):
        pltpu.make_async_copy(v, o, ls.at[i]).wait()

    assert len(names) <= SEMS, len(names)


def hand_over(*refs):
    ins, outs, sems = refs[:4], refs[4:8], refs[8]
    copies = [pltpu.make_async_copy(a, b, sems.at[i]) for i, (a, b) in enumerate(zip(ins, outs))]
    for c in copies:
        c.start()
    for c in copies:
        c.wait()


def per_device(inputs, grad_out, gate_pre, up_pre, gate_weight, up_weight, down_weight):
    scale = 1.0 / math.sqrt(grad_out.shape[0] * lax.axis_size("row"))
    vm = pltpu.VMEM
    anywhere = pl.BlockSpec(memory_space=pl.ANY)
    shapes = (
        jax.ShapeDtypeStruct((32, 512), BF16),
        jax.ShapeDtypeStruct((512, 512), BF16),
        jax.ShapeDtypeStruct((512, 512), BF16),
        jax.ShapeDtypeStruct((512, 512), BF16),
    )
    parts = pl.pallas_call(
        functools.partial(kernel, scale),
        out_shape=shapes,
        in_specs=[anywhere] * 7,
        out_specs=[anywhere] * 4,
        scratch_shapes=[
            vm((8, 2, 2, 32, 512), BF16),
            vm((8, 2, 2, 32, 512), BF16),
            vm((2, 8, 2, 64, 512), BF16),
            vm((8, 128, 512), F32),
            vm((8, 128, 512), F32),
            vm((8, 128, 512), BF16),
            vm((512, 512), BF16),
            vm((512, 512), BF16),
            vm((512, 512), BF16),
            vm((8, 128, 512), F32),
            vm((8, 4, 128, 128), BF16),
            vm((8, 4, 128, 128), BF16),
            vm((8, 128, 128), F32),
            vm((8, 128, 128), F32),
            vm((4, 128, 128), BF16),
            vm((4, 128, 128), BF16),
            vm((4, 128, 128), F32),
            vm((8, 4, 128, 128), BF16),
            vm((8, 128, 512), BF16),
            vm((8, 128, 512), BF16),
            vm((8, 2, 2, 32, 512), F32),
            vm((8, 2, 32, 512), F32),
            vm((16, 32, 512), BF16),
            vm((16, 32, 512), BF16),
            vm((32, 512), F32),
            vm((32, 512), BF16),
            vm((512, 512), BF16),
            vm((512, 512), BF16),
            vm((512, 512), BF16),
            vm((512, 512), BF16),
            vm((512, 512), BF16),
            vm((512, 512), BF16),
            pltpu.SemaphoreType.DMA((9,)),
            pltpu.SemaphoreType.DMA((SEMS,)),
            pltpu.SemaphoreType.DMA((11,)),
        ],
        compiler_params=pltpu.CompilerParams(
            collective_id=0, has_side_effects=True, vmem_limit_bytes=56 * 1024 * 1024
        ),
        name="swiglu_backward",
    )(inputs, grad_out, gate_pre, up_pre, gate_weight, up_weight, down_weight)
    return pl.pallas_call(
        hand_over,
        out_shape=shapes,
        in_specs=[pl.BlockSpec(memory_space=vm)] * 4,
        out_specs=[anywhere] * 4,
        scratch_shapes=[pltpu.SemaphoreType.DMA((4,))],
        name="hand_over",
    )(*parts)


def solution(mesh):
    return jax.shard_map(
        per_device,
        mesh=mesh,
        in_specs=(
            P("row", "col"),
            P("row", "col"),
            P("col", "row"),
            P("col", "row"),
            P("col", "row"),
            P("col", "row"),
            P("row", "col"),
        ),
        out_specs=(P("row", "col"), P("col", "row"), P("col", "row"), P("row", "col")),
        check_vma=False,
    )
```

time: 623 us -> 82.5 us (0.13)
  waiting for transfers between devices: 587 us -> 0 us
  Pallas kernels: 0 us -> 81.7 us
  matrix products: 15.4 us -> 0 us
  between operations: 14.2 us -> 0.64 us
    all_gather x5 -> x0, waiting for transfers between devices: 379 us -> none  [the longest x1 89.3 us: per_device(): lax.all_gather(grad_out, 'row', axis=0, tiled=True)]
    reduce_scatter x2 -> x0, waiting for transfers between devices: 205 us -> none  [the longest x1 128 us: per_device(): lax.psum_scatter(jnp.einsum('tf,df->td', gate_all, gate_weight, preferred...]
    pallas_call x0 -> x2, Pallas kernels: none -> 81.7 us  [the longest x1 79.1 us: per_device(): pl.pallas_call(functools.partial(kernel, scale), out_shape=shapes, in_spe...]
    dot_general x6 -> x0, matrix products: 15.4 us -> none  [the longest x1 3.42 us: per_device(): jnp.einsum('tf,df->td', up_all, up_weight, preferred_element_type=jnp.flo...]
  transfers between devices with their start and end apart: 7 -> 0, of which waited for: 7 -> 0; matrix products, arithmetic and copies ran while one was open for 2% -> 0% of each run, Pallas kernels for 0% -> 0%
where the time goes in v2:
time: 82.5 us; the launch traced here: 82.3 us
  Pallas kernels  81.7 us (99%)
    pallas_call x1, Pallas kernels, per_device(): pl.pallas_call(functools.partial(kernel, scale), out_shape=shapes, in_spe...  79.1 us
    pallas_call x1, Pallas kernels, per_device(): pl.pallas_call(hand_over, out_shape=shapes, in_specs=[pl.BlockSpec(memory...  2.56 us

profile of v2, /device:TPU:24, one launch (start us, length us, event | category | flops | bytes accessed | tf_op | source)
XLA Modules:
  0.0 82.3 jit_solution(10116538078589684882)
XLA Ops:
  0.6 79.1 %swiglu_backward.1 = (bf16[32,512]{1,0:T(8,128)(2,1)}, bf16[512,512]{1,0:T(8,128)(2,1)}, bf16[512,512]{1,0:T(8,128)(2,1)}, bf16[512,512]{1,0:T(8,128)(2,1)}) custom-call(bf16[32,512]{1,0:T(8,128)(2,1)} %inp.1, bf16[32,512]{1,0:T(8,128)(2,1)} %gout.1, bf16[64,512]{1,0:T(8,128)(2,1)} %gpre.1, bf16[64,512]{1,0:T(8,128)(2,1)} %upre.1, bf16[512,512]{1,0:T(8,128)(2,1)} %gw.1, ...), custom_call_target="tpu_custom_call" | custom-call | tf_op jit(solution)/shard_map/swiglu_backward/pallas_call | solution.py:375
  79.8 2.6 %hand_over.1 = (bf16[32,512]{1,0:T(8,128)(2,1)}, bf16[512,512]{1,0:T(8,128)(2,1)}, bf16[512,512]{1,0:T(8,128)(2,1)}, bf16[512,512]{1,0:T(8,128)(2,1)}) custom-call(bf16[32,512]{1,0:T(8,128)(2,1)} %get-tuple-element.8.refs_0_, bf16[512,512]{1,0:T(8,128)(2,1)} %get-tuple-element.9.refs_1_, bf16[512,512]{1,0:T(8,128)(2,1)} %get-tuple-element.10.refs_2_, ...), custom_call_target="tpu_custom_call" | custom-call | tf_op jit(solution)/shard_map/hand_over/pallas_call | solution.py:422

commit v3 on v2

--- a/solution.py
+++ b/solution.py
@@ -11,7 +11,7 @@
 MESH = pl.DeviceIdType.MESH
 F32 = jnp.float32
 BF16 = jnp.bfloat16
-SEMS = 124
+SEMS = 121
 
 
 def mod8(v):
@@ -22,7 +22,7 @@
     scale, inp, gout, gpre, upre, gw, uw, dw,
     o_ig, o_gg, o_ug, o_dg,
     G, X, PRE, A, B, HID, dwt, gwt, uwt, PH, rs_s, rs_r, rl_s, rl_r, xs, xr, S,
-    HG, TG, TU, IG, IGR, ES, ER, ACC, vig, vgg, vug, vdg, vgw, vuw, vdw, ss, rs, ls,
+    HG, TG, TU, IG, IGR, ES, ER, ACC, DG, GG, UG, vgw, vuw, vdw, ss, rs, ls,
 ):
     col = lax.axis_index("col")
     row = lax.axis_index("row")
@@ -73,7 +73,7 @@
     for dev in partners:
         pl.semaphore_signal(bar, inc=1, device_id=dev, device_id_type=MESH)
     loads = [
-        pltpu.make_async_copy(a, b, ls.at[4 + i])
+        pltpu.make_async_copy(a, b, ls.at[i])
         for i, (a, b) in enumerate(
             (
                 (gout, G.at[y, xh, co]),
@@ -88,9 +88,9 @@
     ]
     for c in loads:
         c.start()
+    pl.semaphore_wait(bar, len(partners))
     for c in loads[:4]:
         c.wait()
-    pl.semaphore_wait(bar, len(partners))
 
     yorder = [4, 3, 5, 2, 6, 1, 7]
     need = [4, 3, -3, 2, -2, 1, -1, 0]
@@ -110,13 +110,16 @@
         blk = PRE.at[:, mod8(z + d), xl]
         send(f"px{d}", blk, blk, xlo)
 
-    def pre_hop(k):
+    def pre_recv(k):
         for a in (0, 1):
             for s in (1, -1):
-                n = pre_hops(a, s)
-                if k <= n:
+                if k <= pre_hops(a, s):
                     recv(f"pz{a}{s}{k}", PRE.at[a, mod8(z - s * k), xl])
-                if k < n:
+
+    def pre_next(k):
+        for a in (0, 1):
+            for s in (1, -1):
+                if k < pre_hops(a, s):
                     pre_send(a, s, k + 1)
 
     for a in (0, 1):
@@ -151,9 +154,9 @@
     for c, v, t in zip(loads[4:], (vdw, vgw, vuw), (dwt, gwt, uwt)):
         c.wait()
         t[...] = v[...].T
-    g_row(4)
-    pre_hop(1)
-    for j in need[1:]:
+    pre_recv(1)
+    pre_next(1)
+    for j in need:
         g_row(j)
     pre_x(-1)
     pre_x(1)
@@ -178,7 +181,7 @@
         if k > 1:
             recv(f"r{i}{k - 1}", rs_r.at[i, k - 1])
             val = val + rs_r[i, k - 1].astype(F32)
-        if k == n:
+        if k == 4:
             rl_s[i] = val
             send(f"l{i}", rl_s.at[i], rl_r.at[i], zdev[s])
         else:
@@ -208,13 +211,13 @@
     partial(3)
     partial(-3)
     rs_all(3, 1)
-    pre_hop(2)
     g_sib(2)
     g_sib(-2)
     rs_all(4, 2)
     partial(2)
     partial(-2)
     rs_all(3, 2)
+    pre_recv(2)
     for j in (1, -1, 0):
         g_sib(j)
     pre_x(-2)
@@ -223,7 +226,6 @@
     xpair = X.at[y, :, co]
     for d in yorder:
         copy(xpair, xpair, groups["v"], sem("v"), at_y(mod8(y + d))).start()
-    pre_hop(3)
     rs_all(4, 3)
     partial(1)
     partial(-1)
@@ -231,14 +233,20 @@
     terms(0)
     rs_all(4, 4)
     partial(0)
-    pre_hop(4)
+    pre_next(2)
+    terms(-1)
+    terms(1)
     for q in slices:
         val = PH[z, :, cols(q)]
         for s in (1, -1):
             n = hops(q, s)
             i = streams.index((q, s))
-            recv(f"l{i}", rl_r.at[i])
-            val = val + rl_r[i]
+            if n == 4:
+                recv(f"l{i}", rl_r.at[i])
+                val = val + rl_r[i]
+            else:
+                recv(f"r{i}{n}", rs_r.at[i, n])
+                val = val + rs_r[i, n].astype(F32)
         S[q] = val
         xs[q] = val.astype(BF16)
         send(f"s{q}", xs.at[q], xr.at[q], xlo)
@@ -247,13 +255,17 @@
         blk = HG.at[mod8(z - s * (k - 1)), q]
         send(f"h{streams.index((q, s))}{k}", blk, blk, zdev[s])
 
+    recv("v", X.at[pl.ds(0, 7), 0])
+    send("w", X.at[:, :, co], X.at[:, :, co], sib)
     for q in slices:
         recv(f"s{q}", xr.at[q])
         HG[z, q] = (S[q] + xr[q].astype(F32)).astype(BF16)
         hg_send(q, 1, 1)
         hg_send(q, -1, 1)
-    for d in (-3, 3, 4):
-        pre_x(d)
+    pre_recv(3)
+    pre_next(3)
+    pre_x(-3)
+    pre_x(3)
 
     def block(slot, j):
         t = mod8(z + j)
@@ -294,19 +306,32 @@
 
     order = [0, -1, 1, -2, 2, -3, 3, 4]
 
-    def grads(lhs, rhs, vout, out, i):
+    def grads(*js):
         def body(n, carry):
-            rows = pl.ds(pl.multiple_of(n * 128, 128), 128)
-            acc = lax.dot_general(
-                lhs(rows), rhs(), (((0,), (0,)), ((), ())), preferred_element_type=F32
-            )
-            vout[rows, :] = (acc * scale).astype(BF16)
+            rows = pl.ds(pl.multiple_of(n * 256, 256), 256)
+            tot = [None, None, None]
+            for j in js:
+                t = mod8(z + j)
+                h = HID[t, :, rows]
+                x = X[t, :, :, :, rows].reshape(128, 256)
+                for i, (l, r) in enumerate(((h, G[t].reshape(128, 512)), (x, TG[t]), (x, TU[t]))):
+                    p = lax.dot_general(l, r, (((0,), (0,)), ((), ())), preferred_element_type=F32)
+                    tot[i] = p if tot[i] is None else tot[i] + p
+            for i, (acc, v) in enumerate(zip((DG, GG, UG), (o_dg, o_gg, o_ug))):
+                if js[0] != 0:
+                    tot[i] = tot[i] + acc[rows, :]
+                if js[-1] == 4:
+                    v[rows, :] = (tot[i] * scale).astype(BF16)
+                else:
+                    acc[rows, :] = tot[i]
             return carry
 
-        lax.fori_loop(0, 4, body, 0)
-        pltpu.make_async_copy(vout, out, ls.at[i]).start()
+        lax.fori_loop(0, 2, body, 0)
 
     block(0, 0)
+    recv("w", X.at[:, :, 1 - co])
+    grads(0)
+    out_block(0, 0)
     for k in (1, 2, 3, 4):
         for q, s in streams:
             if k <= hops(q, s):
@@ -315,28 +340,25 @@
                     hg_send(q, s, k + 1)
         mine = (-k, k) if k < 4 else (4,)
         for j in mine:
-            terms(j)
+            if k > 1:
+                terms(j)
+        if k == 2:
+            pre_recv(4)
+            pre_x(4)
         for j in mine:
             block(order.index(j), j)
-        for j in (0,) if k == 1 else (1 - k, k - 1):
+        if k in (2, 3):
+            grads(1 - k, k - 1)
+        for j in mine:
             out_block(order.index(j), j)
-        if k == 3:
-            recv("v", X.at[pl.ds(0, 7), 0])
-            send("w", X.at[:, :, co], X.at[:, :, co], sib)
-    out_block(7, 4)
-
-    x_rows = lambda rows: X[:, :, :, :, rows].reshape(1024, 128)
-    h_rows = lambda rows: HID[:, :, rows].reshape(1024, 128)
-    grads(h_rows, lambda: G[...].reshape(1024, 512), vdg, o_dg, 0)
-    recv("w", X.at[:, :, 1 - co])
-    grads(x_rows, lambda: TG[...].reshape(1024, 512), vgg, o_gg, 1)
-    grads(x_rows, lambda: TU[...].reshape(1024, 512), vug, o_ug, 2)
+
+    grads(-3, 3)
+    grads(4)
     recv("e", ER.at[pl.ds(1, 15)])
     total = ACC[...]
     for i in range(1, 16):
         total = total + ER[i].astype(F32)
-    vig[...] = total.astype(BF16)
-    pltpu.make_async_copy(vig, o_ig, ls.at[3]).start()
+    o_ig[...] = total.astype(BF16)
 
     sent("g", G)
     sent("p", PRE)
@@ -344,12 +366,9 @@
     sent("w", X.at[pl.ds(0, 4)])
     sent("e", ES.at[pl.ds(0, 15)])
     sent("h", HG.at[pl.ds(0, 7)])
-    sent("r", rs_s.at[pl.ds(0, 5)])
+    sent("r", rs_s.at[pl.ds(0, 6)])
     sent("l", rl_s)
     sent("c", IGR)
-    for i, (v, o) in enumerate(((vdg, o_dg), (vgg, o_gg), (vug, o_ug), (vig, o_ig))):
-        pltpu.make_async_copy(v, o, ls.at[i]).wait()
-
     assert len(names) <= SEMS, len(names)
 
 
@@ -374,9 +393,9 @@
     )
     parts = pl.pallas_call(
         functools.partial(kernel, scale),
-        out_shape=shapes,
+        out_shape=tuple(vm(a.shape, a.dtype) for a in shapes),
         in_specs=[anywhere] * 7,
-        out_specs=[anywhere] * 4,
+        out_specs=[pl.BlockSpec(memory_space=vm)] * 4,
         scratch_shapes=[
             vm((8, 2, 2, 32, 512), BF16),
             vm((8, 2, 2, 32, 512), BF16),
@@ -390,8 +409,8 @@
             vm((8, 128, 512), F32),
             vm((8, 4, 128, 128), BF16),
             vm((8, 4, 128, 128), BF16),
-            vm((8, 128, 128), F32),
-            vm((8, 128, 128), F32),
+            vm((4, 128, 128), F32),
+            vm((4, 128, 128), F32),
             vm((4, 128, 128), BF16),
             vm((4, 128, 128), BF16),
             vm((4, 128, 128), F32),
@@ -403,16 +422,15 @@
             vm((16, 32, 512), BF16),
             vm((16, 32, 512), BF16),
             vm((32, 512), F32),
-            vm((32, 512), BF16),
-            vm((512, 512), BF16),
-            vm((512, 512), BF16),
-            vm((512, 512), BF16),
+            vm((512, 512), F32),
+            vm((512, 512), F32),
+            vm((512, 512), F32),
             vm((512, 512), BF16),
             vm((512, 512), BF16),
             vm((512, 512), BF16),
             pltpu.SemaphoreType.DMA((9,)),
             pltpu.SemaphoreType.DMA((SEMS,)),
-            pltpu.SemaphoreType.DMA((11,)),
+            pltpu.SemaphoreType.DMA((7,)),
         ],
         compiler_params=pltpu.CompilerParams(
             collective_id=0, has_side_effects=True, vmem_limit_bytes=56 * 1024 * 1024
@@ -426,7 +444,7 @@
         out_specs=[anywhere] * 4,
         scratch_shapes=[pltpu.SemaphoreType.DMA((4,))],
         name="hand_over",
-    )(*parts)
+    )(*[pltpu.with_memory_space_constraint(p, pltpu.VMEM) for p in parts])
 
 
 def solution(mesh):

time: 82.5 us -> 76.9 us (0.932)
  Pallas kernels: 81.7 us -> 76.2 us
    pallas_call x1, Pallas kernels: 79.1 us -> 75 us  [per_device(): pl.pallas_call(functools.partial(kernel, scale), out_shape=tuple((vm(a.sh...]
    pallas_call x1, Pallas kernels: 2.56 us -> 1.19 us  [per_device(): pl.pallas_call(hand_over, out_shape=shapes, in_specs=[pl.BlockSpec(memory...]
where the time goes in v3:
time: 76.9 us; the launch traced here: 76.8 us
  Pallas kernels  76.2 us (99%)
    pallas_call x1, Pallas kernels, per_device(): pl.pallas_call(functools.partial(kernel, scale), out_shape=tuple((vm(a.sh...  75 us

profile of v3, /device:TPU:24, one launch (start us, length us, event | category | flops | bytes accessed | tf_op | source)
XLA Modules:
  0.0 76.8 jit_solution(13576930253179780973)
XLA Ops:
  0.6 75.0 %swiglu_backward.1 = (bf16[32,512]{1,0:T(8,128)(2,1)S(1)}, bf16[512,512]{1,0:T(8,128)(2,1)S(1)}, bf16[512,512]{1,0:T(8,128)(2,1)S(1)}, bf16[512,512]{1,0:T(8,128)(2,1)S(1)}) custom-call(bf16[32,512]{1,0:T(8,128)(2,1)} %inp.1, bf16[32,512]{1,0:T(8,128)(2,1)} %gout.1, bf16[64,512]{1,0:T(8,128)(2,1)} %gpre.1, bf16[64,512]{1,0:T(8,128)(2,1)} %upre.1, ...), custom_call_target="tpu_custom_call" | custom-call | tf_op jit(solution)/shard_map/swiglu_backward/pallas_call | solution.py:394
  75.6 1.2 %hand_over.1 = (bf16[32,512]{1,0:T(8,128)(2,1)}, bf16[512,512]{1,0:T(8,128)(2,1)}, bf16[512,512]{1,0:T(8,128)(2,1)}, bf16[512,512]{1,0:T(8,128)(2,1)}) custom-call(bf16[32,512]{1,0:T(8,128)(2,1)S(1)} %get-tuple-element.8.refs_0_, bf16[512,512]{1,0:T(8,128)(2,1)S(1)} %get-tuple-element.9.refs_1_, bf16[512,512]{1,0:T(8,128)(2,1)S(1)} %get-tuple-element.10.refs_2_, ...), custom_call_target="tpu_custom_call" | custom-call | tf_op jit(solution)/shard_map/hand_over/pallas_call | solution.py:440

commit v4 on v3

--- a/solution.py
+++ b/solution.py
@@ -21,8 +21,8 @@
 def kernel(
     scale, inp, gout, gpre, upre, gw, uw, dw,
     o_ig, o_gg, o_ug, o_dg,
-    G, X, PRE, A, B, HID, dwt, gwt, uwt, PH, rs_s, rs_r, rl_s, rl_r, xs, xr, S,
-    HG, TG, TU, IG, IGR, ES, ER, ACC, DG, GG, UG, vgw, vuw, vdw, ss, rs, ls,
+    G, X, PRE, A, B, HT, XT, dwt, gwt, uwt, PH, rs_s, rs_r, rl_s, rl_r, xs, xr, S,
+    HG, TG, TU, IG, IGR, ES, ER, ACC, vgw, vuw, vdw, ss, rs, ls,
 ):
     col = lax.axis_index("col")
     row = lax.axis_index("row")
@@ -110,16 +110,12 @@
         blk = PRE.at[:, mod8(z + d), xl]
         send(f"px{d}", blk, blk, xlo)
 
-    def pre_recv(k):
+    def pre_hop(k, get=True, put=True):
         for a in (0, 1):
             for s in (1, -1):
-                if k <= pre_hops(a, s):
+                if get and k <= pre_hops(a, s):
                     recv(f"pz{a}{s}{k}", PRE.at[a, mod8(z - s * k), xl])
-
-    def pre_next(k):
-        for a in (0, 1):
-            for s in (1, -1):
-                if k < pre_hops(a, s):
+                if put and k < pre_hops(a, s):
                     pre_send(a, s, k + 1)
 
     for a in (0, 1):
@@ -154,12 +150,14 @@
     for c, v, t in zip(loads[4:], (vdw, vgw, vuw), (dwt, gwt, uwt)):
         c.wait()
         t[...] = v[...].T
-    pre_recv(1)
-    pre_next(1)
+    pre_hop(1)
+    other = PRE.at[:, z, 1 - xl]
+    recv("px0", other)
+    for s in (1, -1):
+        send(f"py{s}", other, other, zdev[s])
     for j in need:
         g_row(j)
-    pre_x(-1)
-    pre_x(1)
+    pre_hop(2)
     for j in need[:3]:
         g_sib(j)
 
@@ -168,7 +166,8 @@
     def hops(q, s):
         return 4 if (q < 2) == (s == 1) else 3
 
-    streams = [(q, s) for n in (4, 3) for q in slices for s in (1, -1) if hops(q, s) == n]
+    mixed = [0, 2, 1, 3]
+    streams = [(q, s) for n in (4, 3) for q in mixed for s in (1, -1) if hops(q, s) == n]
 
     def cols(q):
         return pl.ds(q * 128, 128)
@@ -193,9 +192,13 @@
             if hops(q, s) == n:
                 rs_step(q, s, k)
 
+    def tokens(t):
+        return pl.ds(pl.multiple_of(t * 128, 128), 128)
+
     def terms(j):
         t = mod8(z + j)
-        recv(f"px{j}", PRE.at[:, t, 1 - xl])
+        if j:
+            recv(f"py{-j}" if j in (1, -1) else f"px{j}", PRE.at[:, t, 1 - xl])
         for h in (0, 1):
             c = pl.ds(h * 256, 256)
             g = PRE[0, t, :, :, c].reshape(128, 256).astype(F32)
@@ -203,7 +206,7 @@
             sg = 1.0 / (1.0 + jnp.exp(-g))
             silu = g * sg
             A[t, :, c] = silu
-            HID[t, :, c] = (silu * u).astype(BF16)
+            HT[c, tokens(t)] = (silu * u).astype(BF16).T
             B[t, :, c] = u * sg * (1.0 + g * (1.0 - sg))
 
     partial(4)
@@ -211,17 +214,16 @@
     partial(3)
     partial(-3)
     rs_all(3, 1)
+    pre_x(-2)
+    pre_x(2)
     g_sib(2)
     g_sib(-2)
     rs_all(4, 2)
     partial(2)
     partial(-2)
     rs_all(3, 2)
-    pre_recv(2)
     for j in (1, -1, 0):
         g_sib(j)
-    pre_x(-2)
-    pre_x(2)
     recv("xx", X.at[y, 1 - xh, co])
     xpair = X.at[y, :, co]
     for d in yorder:
@@ -229,14 +231,17 @@
     rs_all(4, 3)
     partial(1)
     partial(-1)
+    pre_hop(3, put=False)
+    pre_x(-3)
+    pre_x(3)
     rs_all(3, 3)
     terms(0)
     rs_all(4, 4)
     partial(0)
-    pre_next(2)
+    pre_hop(3, get=False)
     terms(-1)
     terms(1)
-    for q in slices:
+    for q in mixed:
         val = PH[z, :, cols(q)]
         for s in (1, -1):
             n = hops(q, s)
@@ -255,17 +260,11 @@
         blk = HG.at[mod8(z - s * (k - 1)), q]
         send(f"h{streams.index((q, s))}{k}", blk, blk, zdev[s])
 
-    recv("v", X.at[pl.ds(0, 7), 0])
-    send("w", X.at[:, :, co], X.at[:, :, co], sib)
-    for q in slices:
+    for q in mixed:
         recv(f"s{q}", xr.at[q])
         HG[z, q] = (S[q] + xr[q].astype(F32)).astype(BF16)
         hg_send(q, 1, 1)
         hg_send(q, -1, 1)
-    pre_recv(3)
-    pre_next(3)
-    pre_x(-3)
-    pre_x(3)
 
     def block(slot, j):
         t = mod8(z + j)
@@ -306,54 +305,63 @@
 
     order = [0, -1, 1, -2, 2, -3, 3, 4]
 
-    def grads(*js):
+    def grad(lhs, rhs, out):
         def body(n, carry):
             rows = pl.ds(pl.multiple_of(n * 256, 256), 256)
-            tot = [None, None, None]
-            for j in js:
-                t = mod8(z + j)
-                h = HID[t, :, rows]
-                x = X[t, :, :, :, rows].reshape(128, 256)
-                for i, (l, r) in enumerate(((h, G[t].reshape(128, 512)), (x, TG[t]), (x, TU[t]))):
-                    p = lax.dot_general(l, r, (((0,), (0,)), ((), ())), preferred_element_type=F32)
-                    tot[i] = p if tot[i] is None else tot[i] + p
-            for i, (acc, v) in enumerate(zip((DG, GG, UG), (o_dg, o_gg, o_ug))):
-                if js[0] != 0:
-                    tot[i] = tot[i] + acc[rows, :]
-                if js[-1] == 4:
-                    v[rows, :] = (tot[i] * scale).astype(BF16)
-                else:
-                    acc[rows, :] = tot[i]
+            acc = jnp.dot(lhs[rows, :], rhs[...].reshape(1024, 512), preferred_element_type=F32)
+            out[rows, :] = (acc * scale).astype(BF16)
             return carry
 
         lax.fori_loop(0, 2, body, 0)
 
-    block(0, 0)
+    def hop(n, k):
+        for q, s in streams:
+            if hops(q, s) == n:
+                recv(f"h{streams.index((q, s))}{k}", HG.at[mod8(z - s * k), q])
+                if k < n:
+                    hg_send(q, s, k + 1)
+
+    def blocks(*js):
+        for j in js:
+            block(order.index(j), j)
+
+    def outs(*js):
+        for j in js:
+            out_block(order.index(j), j)
+
+    blocks(0)
+    hop(4, 1)
+    terms(-2)
+    terms(2)
+    outs(0)
+    hop(3, 1)
+    pre_hop(4)
+    pre_x(4)
+    blocks(-1, 1)
+    recv("v", X.at[pl.ds(0, 7), 0])
+    send("w", X.at[:, :, co], X.at[:, :, co], sib)
+    hop(4, 2)
+    outs(-1, 1)
+    hop(3, 2)
+    blocks(-2, 2)
     recv("w", X.at[:, :, 1 - co])
-    grads(0)
-    out_block(0, 0)
-    for k in (1, 2, 3, 4):
-        for q, s in streams:
-            if k <= hops(q, s):
-                recv(f"h{streams.index((q, s))}{k}", HG.at[mod8(z - s * k), q])
-                if k < hops(q, s):
-                    hg_send(q, s, k + 1)
-        mine = (-k, k) if k < 4 else (4,)
-        for j in mine:
-            if k > 1:
-                terms(j)
-        if k == 2:
-            pre_recv(4)
-            pre_x(4)
-        for j in mine:
-            block(order.index(j), j)
-        if k in (2, 3):
-            grads(1 - k, k - 1)
-        for j in mine:
-            out_block(order.index(j), j)
-
-    grads(-3, 3)
-    grads(4)
+    for t in range(8):
+        XT[:, t * 128 : t * 128 + 128] = X[t].reshape(128, 512).T
+    hop(4, 3)
+    outs(-2, 2)
+    hop(3, 3)
+    terms(-3)
+    terms(3)
+    blocks(-3, 3)
+    terms(4)
+    outs(-3, 3)
+    hop(4, 4)
+    blocks(4)
+    outs(4)
+
+    grad(HT, G, o_dg)
+    grad(XT, TG, o_gg)
+    grad(XT, TU, o_ug)
     recv("e", ER.at[pl.ds(1, 15)])
     total = ACC[...]
     for i in range(1, 16):
@@ -402,7 +410,8 @@
             vm((2, 8, 2, 64, 512), BF16),
             vm((8, 128, 512), F32),
             vm((8, 128, 512), F32),
-            vm((8, 128, 512), BF16),
+            vm((512, 1024), BF16),
+            vm((512, 1024), BF16),
             vm((512, 512), BF16),
             vm((512, 512), BF16),
             vm((512, 512), BF16),
@@ -422,9 +431,6 @@
             vm((16, 32, 512), BF16),
             vm((16, 32, 512), BF16),
             vm((32, 512), F32),
-            vm((512, 512), F32),
-            vm((512, 512), F32),
-            vm((512, 512), F32),
             vm((512, 512), BF16),
             vm((512, 512), BF16),
             vm((512, 512), BF16),

time: 76.9 us -> 74.8 us (0.973)
  Pallas kernels: 76.2 us -> 73.8 us
    pallas_call x1, Pallas kernels: 75 us -> 72.6 us  [per_device(): pl.pallas_call(functools.partial(kernel, scale), out_shape=tuple((vm(a.sh...]
where the time goes in v4:
time: 74.8 us; the launch traced here: 74.4 us
  Pallas kernels  73.8 us (99%)
    pallas_call x1, Pallas kernels, per_device(): pl.pallas_call(functools.partial(kernel, scale), out_shape=tuple((vm(a.sh...  72.6 us

profile of v4, /device:TPU:24, one launch (start us, length us, event | category | flops | bytes accessed | tf_op | source)
XLA Modules:
  0.0 74.4 jit_solution(9112507864390409012)
XLA Ops:
  0.6 72.6 %swiglu_backward.1 = (bf16[32,512]{1,0:T(8,128)(2,1)S(1)}, bf16[512,512]{1,0:T(8,128)(2,1)S(1)}, bf16[512,512]{1,0:T(8,128)(2,1)S(1)}, bf16[512,512]{1,0:T(8,128)(2,1)S(1)}) custom-call(bf16[32,512]{1,0:T(8,128)(2,1)} %inp.1, bf16[32,512]{1,0:T(8,128)(2,1)} %gout.1, bf16[64,512]{1,0:T(8,128)(2,1)} %gpre.1, bf16[64,512]{1,0:T(8,128)(2,1)} %upre.1, ...), custom_call_target="tpu_custom_call" | custom-call | tf_op jit(solution)/shard_map/swiglu_backward/pallas_call | solution.py:402
  73.2 1.2 %hand_over.1 = (bf16[32,512]{1,0:T(8,128)(2,1)}, bf16[512,512]{1,0:T(8,128)(2,1)}, bf16[512,512]{1,0:T(8,128)(2,1)}, bf16[512,512]{1,0:T(8,128)(2,1)}) custom-call(bf16[32,512]{1,0:T(8,128)(2,1)S(1)} %get-tuple-element.8.refs_0_, bf16[512,512]{1,0:T(8,128)(2,1)S(1)} %get-tuple-element.9.refs_1_, bf16[512,512]{1,0:T(8,128)(2,1)S(1)} %get-tuple-element.10.refs_2_, ...), custom_call_target="tpu_custom_call" | custom-call | tf_op jit(solution)/shard_map/hand_over/pallas_call | solution.py:446

commit v5 on v4

--- a/solution.py
+++ b/solution.py
@@ -11,7 +11,7 @@
 MESH = pl.DeviceIdType.MESH
 F32 = jnp.float32
 BF16 = jnp.bfloat16
-SEMS = 121
+SEMS = 124
 
 
 def mod8(v):
@@ -67,7 +67,8 @@
         recv_at(sem(name), dst)
 
     bar = pltpu.get_barrier_semaphore()
-    partners = [zdev[1], zdev[-1], xlo, xhi, sib]
+    across = {"col": col, "row": y * 4 + (1 - xh) * 2 + 1 - co}
+    partners = [zdev[1], zdev[-1], xlo, xhi, sib, across]
     partners += [at_y(mod8(y + d)) for d in range(1, 8)]
     partners += [at_y(mod8(y + d), 1 - xh) for d in range(1, 8)]
     for dev in partners:
@@ -94,6 +95,7 @@
 
     yorder = [4, 3, 5, 2, 6, 1, 7]
     need = [4, 3, -3, 2, -2, 1, -1, 0]
+    first = [4, 3, -3]
     own = G.at[y, xh, co]
     g0 = [sem(f"gy{d}") for d in range(8)][0]
     for d in yorder:
@@ -132,8 +134,13 @@
 
         blk = G.at[t, xh, co]
         send(f"gx{j}", blk, blk, xhi)
+        if j in first:
+            send(f"gz{j}", blk, blk, across)
+            send(f"gs{j}", blk, blk, sib)
 
     def g_sib(j):
+        if j in first:
+            return
         t = mod8(z + j)
         recv(f"gx{j}", G.at[t, 1 - xh, co])
         blk = G.at[t, :, co]
@@ -141,7 +148,12 @@
 
     def partial(j):
         t = mod8(z + j)
-        recv(f"gs{j}", G.at[t, :, 1 - co])
+        if j in first:
+            recv(f"gs{j}", G.at[t, xh, 1 - co])
+            recv(f"gx{j}", G.at[t, 1 - xh, co])
+            recv(f"gz{j}", G.at[t, 1 - xh, 1 - co])
+        else:
+            recv(f"gs{j}", G.at[t, :, 1 - co])
         PH[t] = jnp.dot(G[t].reshape(128, 512), dwt[...], preferred_element_type=F32)
 
     xown = X.at[y, xh, co]
@@ -155,7 +167,7 @@
     recv("px0", other)
     for s in (1, -1):
         send(f"py{s}", other, other, zdev[s])
-    for j in need:
+    for j in need[:5]:
         g_row(j)
     pre_hop(2)
     for j in need[:3]:
@@ -211,6 +223,8 @@
 
     partial(4)
     rs_all(4, 1)
+    for j in need[5:]:
+        g_row(j)
     partial(3)
     partial(-3)
     rs_all(3, 1)

time: 74.8 us -> 73.7 us (0.985)
  the two profiles are of different devices: /device:TPU:24 before, /device:TPU:33 now
where the time goes in v5:
time: 73.7 us; the launch traced here: 73.6 us
  Pallas kernels  72.9 us (99%)
    pallas_call x1, Pallas kernels, per_device(): pl.pallas_call(functools.partial(kernel, scale), out_shape=tuple((vm(a.sh...  71.7 us

profile of v5, /device:TPU:33, one launch (start us, length us, event | category | flops | bytes accessed | tf_op | source)
XLA Modules:
  0.0 73.6 jit_solution(9107527223440572050)
XLA Ops:
  0.6 71.7 %swiglu_backward.1 = (bf16[32,512]{1,0:T(8,128)(2,1)S(1)}, bf16[512,512]{1,0:T(8,128)(2,1)S(1)}, bf16[512,512]{1,0:T(8,128)(2,1)S(1)}, bf16[512,512]{1,0:T(8,128)(2,1)S(1)}) custom-call(bf16[32,512]{1,0:T(8,128)(2,1)} %inp.1, bf16[32,512]{1,0:T(8,128)(2,1)} %gout.1, bf16[64,512]{1,0:T(8,128)(2,1)} %gpre.1, bf16[64,512]{1,0:T(8,128)(2,1)} %upre.1, ...), custom_call_target="tpu_custom_call" | custom-call | tf_op jit(solution)/shard_map/swiglu_backward/pallas_call | solution.py:416
  72.4 1.2 %hand_over.1 = (bf16[32,512]{1,0:T(8,128)(2,1)}, bf16[512,512]{1,0:T(8,128)(2,1)}, bf16[512,512]{1,0:T(8,128)(2,1)}, bf16[512,512]{1,0:T(8,128)(2,1)}) custom-call(bf16[32,512]{1,0:T(8,128)(2,1)S(1)} %get-tuple-element.8.refs_0_, bf16[512,512]{1,0:T(8,128)(2,1)S(1)} %get-tuple-element.9.refs_1_, bf16[512,512]{1,0:T(8,128)(2,1)S(1)} %get-tuple-element.10.refs_2_, ...), custom_call_target="tpu_custom_call" | custom-call | tf_op jit(solution)/shard_map/hand_over/pallas_call | solution.py:460

commit v6 on v5

--- a/solution.py
+++ b/solution.py
@@ -238,6 +238,9 @@
     rs_all(3, 2)
     for j in (1, -1, 0):
         g_sib(j)
+    pre_hop(3, put=False)
+    pre_x(-3)
+    pre_x(3)
     recv("xx", X.at[y, 1 - xh, co])
     xpair = X.at[y, :, co]
     for d in yorder:
@@ -245,9 +248,6 @@
     rs_all(4, 3)
     partial(1)
     partial(-1)
-    pre_hop(3, put=False)
-    pre_x(-3)
-    pre_x(3)
     rs_all(3, 3)
     terms(0)
     rs_all(4, 4)

time: 73.7 us -> 73.8 us (level)
  no operation moved by 1% of the time
where the time goes in v6:
time: 73.8 us; the launch traced here: 73.6 us
  Pallas kernels  73 us (99%)
    pallas_call x1, Pallas kernels, per_device(): pl.pallas_call(functools.partial(kernel, scale), out_shape=tuple((vm(a.sh...  71.8 us

profile of v6, /device:TPU:33, one launch (start us, length us, event | category | flops | bytes accessed | tf_op | source)
XLA Modules:
  0.0 73.6 jit_solution(3812841272965036407)
XLA Ops:
  0.6 71.8 %swiglu_backward.1 = (bf16[32,512]{1,0:T(8,128)(2,1)S(1)}, bf16[512,512]{1,0:T(8,128)(2,1)S(1)}, bf16[512,512]{1,0:T(8,128)(2,1)S(1)}, bf16[512,512]{1,0:T(8,128)(2,1)S(1)}) custom-call(bf16[32,512]{1,0:T(8,128)(2,1)} %inp.1, bf16[32,512]{1,0:T(8,128)(2,1)} %gout.1, bf16[64,512]{1,0:T(8,128)(2,1)} %gpre.1, bf16[64,512]{1,0:T(8,128)(2,1)} %upre.1, ...), custom_call_target="tpu_custom_call" | custom-call | tf_op jit(solution)/shard_map/swiglu_backward/pallas_call | solution.py:416
  72.5 1.2 %hand_over.1 = (bf16[32,512]{1,0:T(8,128)(2,1)}, bf16[512,512]{1,0:T(8,128)(2,1)}, bf16[512,512]{1,0:T(8,128)(2,1)}, bf16[512,512]{1,0:T(8,128)(2,1)}) custom-call(bf16[32,512]{1,0:T(8,128)(2,1)S(1)} %get-tuple-element.8.refs_0_, bf16[512,512]{1,0:T(8,128)(2,1)S(1)} %get-tuple-element.9.refs_1_, bf16[512,512]{1,0:T(8,128)(2,1)S(1)} %get-tuple-element.10.refs_2_, ...), custom_call_target="tpu_custom_call" | custom-call | tf_op jit(solution)/shard_map/hand_over/pallas_call | solution.py:460
